TPU v7x, 32 devices: a whole 2x2x4 slice. The times are simulated.
32 devices in a mesh: grp: 2 (over core), seq: 4 (over y, x), row: 4 (over z).
Axes of the slice: x: 2, y: 2, z: 4, core: 2. Of those that a mesh axis runs over, the one named last changes fastest.
Arguments:
- tokens: bfloat16 [512, 70, 1150], P(('grp', 'seq')), may hold values from -6 to 6
- in_mask: int32 [512, 1150], P(('grp', 'seq')), may hold values 0 or 1
- out_mask: int32 [512, 400], P(('grp', 'seq')), may hold values 0 or 1
- lengths: int32 [512], P(('grp', 'seq')), may hold values from 35 to 70, as said below
- groups: int32 [512], P(('grp', 'seq')), may hold values from 0 to 1, as said below
- input_gate_weight: bfloat16 [1600, 1150], P('row'), may hold values from -0.1875 to 0.1875
- w_recur: bfloat16 [1600, 400], P('row'), may hold values from -0.3125 to 0.3125
- weight_mask: int32 [1600, 400], P('row'), may hold values 0 or 1
- bias: float32 [1600], P('row'), may hold values from -3 to 3
- cotangent: bfloat16 [512, 70, 400], P(('grp', 'seq')), may hold values from -6 to 6
Outputs:
- input_grad: float32 [512, 70, 1150], P(('grp', 'seq', 'row'))
- grad_input_weight: float32 [2, 1600, 1150], P('grp', 'row')
- grad_recur_weight: float32 [2, 1600, 400], P('grp', 'row')
- grad_bias: float32 [2, 1600], P('grp', 'row')
- gram: float32 [2, 2], replicated
Inputs may be any that keep to these rules, and one draw needn't show every extreme that they name: `lengths`: each sequence has the full length or fewer steps; some sequence of the batch has exactly 70 steps and some exactly 35. Both groups have sequences.
All inputs are finite; a program needn't handle non-finite values. No bound on the sum of `in_mask` or of `out_mask` or of `weight_mask` on one device may be relied on, other than what follows from the above.
Results may differ from a plain program's by a relative error of at most 0.0063.
Values may be sent and summed in bfloat16 or wider, within the bound.
No kernel may reach another device: no remote copies, remote signals or barrier semaphores. Data moves between devices by JAX's collectives and lax.ppermute only.
A program may use at most 256 MiB of HBM per device.

v0:
```python
import jax
import jax.numpy as jnp
from jax import lax
from jax.sharding import PartitionSpec as P

ACTIVATION_COEF = 2.0
TAR_BETA = 1.0
KEEP_INPUT = 0.75
KEEP_OUTPUT = 0.6
KEEP_WEIGHT = 0.5


def swapped(block, axis, stride):
    count = lax.axis_size(axis)
    route = []
    for low in range(count):
        high = low | 1 << stride
        if high != low and high < count:
            route += [(low, high), (high, low)]
    return lax.ppermute(block, axis, route)


def gate_split(values, hidden):
    return (
        jax.nn.sigmoid(values[:, :hidden]),
        jax.nn.sigmoid(values[:, hidden : 2 * hidden]),
        jnp.tanh(values[:, 2 * hidden : 3 * hidden]),
        jax.nn.sigmoid(values[:, 3 * hidden :]),
    )


def local(
    tokens,
    in_mask,
    out_mask,
    lengths,
    groups,
    input_gate_weight,
    w_recur,
    weight_mask,
    bias,
    cotangent,
):
    seq_count, time_steps, width_in = tokens.shape
    hidden = cotangent.shape[2]
    row_count = input_gate_weight.shape[0]
    row_start = lax.axis_index("row") * row_count
    share = seq_count // lax.axis_size("row")
    share_start = lax.axis_index("row") * share
    group_hot = (groups[:, None] == jnp.arange(2)[None, :]).astype(jnp.float32)
    valid_mask = (jnp.arange(time_steps)[None, :] < lengths[:, None]).astype(jnp.float32)
    local_counts = jnp.sum(group_hot * jnp.sum(valid_mask, 1)[:, None], 0)
    counts = lax.psum(local_counts, ("grp", "seq"))
    group_ratio = jnp.sum(counts) / counts
    seq_ratio = jnp.sum(group_hot * group_ratio[None, :], 1)
    in_scale = in_mask.astype(jnp.float32) / KEEP_INPUT
    dropped_weight = (tokens.astype(jnp.float32) * in_scale[:, None, :]).astype(jnp.bfloat16)
    w_scale = weight_mask.astype(jnp.float32) / KEEP_WEIGHT
    w_eff = (w_recur.astype(jnp.float32) * w_scale).astype(jnp.bfloat16)
    projected = (
        jnp.einsum(
            "thw,aw->hta", dropped_weight, input_gate_weight, preferred_element_type=jnp.float32
        )
        + bias[None, None, :]
    )
    zero_state = jnp.zeros((seq_count, hidden), jnp.float32)

    def full_gates(proj_step, hidden_low):
        partial_gates = proj_step + jnp.einsum(
            "sh,rh->sr", hidden_low, w_eff, preferred_element_type=jnp.float32
        )
        return lax.all_gather(partial_gates, "row", axis=1, tiled=True)

    def recur_back(pre_grad):
        own_rows = lax.dynamic_slice_in_dim(pre_grad, row_start, row_count, 1)
        partial_back = jnp.dot(own_rows, w_eff, preferred_element_type=jnp.float32)
        return lax.psum(partial_back, "row")

    def forward_step(carry, proj_step):
        cell_state, hidden_low = carry
        pre_act = full_gates(proj_step, hidden_low)
        gate_input_part, gate_forget, gate_cell, gate_output_part = gate_split(pre_act, hidden)
        new_cell = gate_forget * cell_state + gate_input_part * gate_cell
        new_hidden = gate_output_part * jnp.tanh(new_cell)
        stored = jnp.concatenate([gate_input_part, gate_forget, gate_cell, gate_output_part], 1)
        return ((new_cell, new_hidden.astype(jnp.bfloat16)), (stored, new_cell, new_hidden))

    start_state = (zero_state, zero_state.astype(jnp.bfloat16))
    _, (activations, cell_seq, hidden_seq) = lax.scan(forward_step, start_state, projected)
    out_scale = out_mask.astype(jnp.float32) / KEEP_OUTPUT
    cot_time = jnp.swapaxes(cotangent, 0, 1).astype(jnp.float32)
    valid_time = valid_mask.T
    outputs = hidden_seq * out_scale[None]
    out_grad = valid_time[:, :, None] * (
        cot_time + 2.0 * ACTIVATION_COEF * seq_ratio[None, :, None] * outputs
    )
    zero_row = jnp.zeros((1, seq_count, hidden), jnp.float32)
    hidden_prev = jnp.concatenate([zero_row, hidden_seq[:-1]], 0)
    later = (jnp.arange(time_steps) >= 1).astype(jnp.float32)
    smooth_weight = 2.0 * TAR_BETA * seq_ratio[None, :] * valid_time * later[:, None]
    smooth_term = smooth_weight[:, :, None] * (hidden_seq - hidden_prev)
    direct_grad = (
        out_grad * out_scale[None] + smooth_term - jnp.concatenate([smooth_term[1:], zero_row], 0)
    )
    cell_prev = jnp.concatenate([zero_row, cell_seq[:-1]], 0)

    def backward_step(carry, inputs_now):
        cell_grad, recur_grad = carry
        direct_now, stored, cell_state, cell_before = inputs_now
        gate_input_part = stored[:, :hidden]
        gate_forget = stored[:, hidden : 2 * hidden]
        gate_cell = stored[:, 2 * hidden : 3 * hidden]
        gate_output_part = stored[:, 3 * hidden :]
        hidden_grad = direct_now + recur_grad
        tanh_cell = jnp.tanh(cell_state)
        total_cell = cell_grad + hidden_grad * gate_output_part * (1.0 - tanh_cell * tanh_cell)
        pre_grad = jnp.concatenate(
            [
                total_cell * gate_cell * gate_input_part * (1.0 - gate_input_part),
                total_cell * cell_before * gate_forget * (1.0 - gate_forget),
                total_cell * gate_input_part * (1.0 - gate_cell * gate_cell),
                hidden_grad * tanh_cell * gate_output_part * (1.0 - gate_output_part),
            ],
            1,
        ).astype(jnp.bfloat16)
        own_rows = lax.dynamic_slice_in_dim(pre_grad, row_start, row_count, 1)
        share_rows = lax.dynamic_slice_in_dim(pre_grad, share_start, share, 0)
        new_carry = (total_cell * gate_forget, recur_back(pre_grad))
        return (new_carry, (own_rows, share_rows[:, :0]))

    _, (pre_grads, share_grads) = lax.scan(
        backward_step,
        (zero_state, zero_state),
        (direct_grad, activations, cell_seq, cell_prev),
        reverse=True,
    )
    grad_seq = jnp.swapaxes(pre_grads, 0, 1)
    prev_low = jnp.swapaxes(hidden_prev, 0, 1).astype(jnp.bfloat16)
    grads_in = []
    grads_rec = []
    bias_gradient_rows = []
    for group_index in range(2):
        selector = (groups == group_index).astype(jnp.bfloat16)
        masked = grad_seq * selector[:, None, None]
        grads_in.append(
            jnp.einsum("slr,slk->rk", masked, dropped_weight, preferred_element_type=jnp.float32)
        )
        grads_rec.append(
            jnp.einsum("slr,slh->rh", masked, prev_low, preferred_element_type=jnp.float32)
            * w_scale
        )
        bias_gradient_rows.append(jnp.sum(masked.astype(jnp.float32), (0, 1)))
    stacked = (jnp.stack(grads_in), jnp.stack(grads_rec), jnp.stack(bias_gradient_rows))
    own_scale = lax.dynamic_slice_in_dim(in_scale, share_start, share, 0)
    input_sum = lax.psum_scatter(
        jnp.einsum("slr,rk->slk", grad_seq, input_gate_weight, preferred_element_type=jnp.float32),
        "row",
        scatter_dimension=0,
        tiled=True,
    )
    input_grad = input_sum * own_scale[:, None, :]
    own_grads = (
        lax.psum_scatter(stacked[0], "grp", scatter_dimension=0, tiled=True),
        lax.psum_scatter(stacked[1], "grp", scatter_dimension=0, tiled=True),
        lax.psum_scatter(stacked[2], "grp", scatter_dimension=0, tiled=True),
    )
    own_grads = lax.psum((own_grads[0], own_grads[1], own_grads[2]), "seq")
    flat_own = jnp.concatenate([member.reshape(-1) for member in own_grads])
    flat_peer = swapped(flat_own.astype(jnp.bfloat16), "grp", 0).astype(flat_own.dtype)
    self_dot = jnp.sum(flat_own * flat_own)
    cross_dot = jnp.sum(flat_own * flat_peer)
    mine_hot = (jnp.arange(2) == lax.axis_index("grp")).astype(jnp.float32)
    local_gram = (
        mine_hot[:, None] * mine_hot[None, :] * self_dot
        + mine_hot[:, None] * (1.0 - mine_hot)[None, :] * cross_dot
    )
    gram = lax.psum(local_gram, ("grp", "row"))
    grad_in, grad_rec, grad_bias = own_grads
    return (input_grad, grad_in, grad_rec, grad_bias, gram)


def solution(mesh):
    return jax.shard_map(
        local,
        mesh=mesh,
        in_specs=(
            P(("grp", "seq"), None, None),
            P(("grp", "seq"), None),
            P(("grp", "seq"), None),
            P(("grp", "seq")),
            P(("grp", "seq")),
            P("row", None),
            P("row", None),
            P("row", None),
            P("row"),
            P(("grp", "seq"), None, None),
        ),
        out_specs=(
            P(("grp", "seq", "row"), None, None),
            P("grp", "row", None),
            P("grp", "row", None),
            P("grp", "row"),
            P(),
        ),
        check_vma=False,
    )
```

profile of v0, /device:TPU:0, one launch (start us, length us, event | category | flops | bytes accessed | tf_op | source)
XLA Modules:
  0.0 4704.8 jit_solution(5779984104247842560)
XLA Ops:
  33.6 1464.2 %while.38 = (s32[]{:T(128)}, f32[64,400]{1,0:T(8,128)S(1)}, bf16[64,400]{1,0:T(8,128)(2,1)S(1)}, f32[70,64,1600]{2,1,0:T(8,128)}, f32[70,64,400]{2,1,0:T(8,128)}...) while((s32[]{:T(128)}, f32[64,400]{1,0:T(8,128)S(1)}, ...), condition=%wide.region_6.7_spmd.clone, body=%wide.region_5.6_spmd.clone.sunk | while | flops 21171204 | bytes 6539380 | solution.py:89
  1561.2 2708.6 %while.39 = (s32[]{:T(128)}, f32[64,400]{1,0:T(8,128)S(1)}, f32[64,400]{1,0:T(8,128)}, bf16[70,64,400]{2,1,0:T(8,128)(2,1)}, f32[70,64,400]{2,1,0:T(8,128)}, /*i...) while((s32[]{:T(128)}, f32[64,400]{1,0:T(8,128)S(1)}, ...), condition=%wide.region_9.10_spmd.clone, body=%wide.region_7.9_spmd.clone.sunk | while | flops 21222404 | bytes 4233935 | solution.py:131
  1566.3 35.4 all-reduce.10.cloned.1.call-done
  1645.4 33.6 all-reduce.10.cloned.1.call-done
  1800.1 33.6 all-reduce.10.cloned.1.call-done
  1877.4 33.6 all-reduce.10.cloned.1.call-done
  1954.8 33.6 all-reduce.10.cloned.1.call-done
  1993.4 33.6 all-reduce.10.cloned.1.call-done
  2109.4 33.6 all-reduce.10.cloned.1.call-done
  2264.1 33.6 all-reduce.10.cloned.1.call-done
  2418.8 33.6 all-reduce.10.cloned.1.call-done
  2457.5 33.6 all-reduce.10.cloned.1.call-done
  2496.1 33.6 all-reduce.10.cloned.1.call-done
  2573.5 33.6 all-reduce.10.cloned.1.call-done
  2612.1 33.6 all-reduce.10.cloned.1.call-done
  2728.1 33.6 all-reduce.10.cloned.1.call-done
  2882.8 33.6 all-reduce.10.cloned.1.call-done
  2960.2 33.6 all-reduce.10.cloned.1.call-done
  3037.5 33.6 all-reduce.10.cloned.1.call-done
  3076.2 33.6 all-reduce.10.cloned.1.call-done
  3114.9 33.6 all-reduce.10.cloned.1.call-done
  3192.2 33.6 all-reduce.10.cloned.1.call-done
  3230.9 33.6 all-reduce.10.cloned.1.call-done
  3346.9 33.6 all-reduce.10.cloned.1.call-done
  3501.5 33.6 all-reduce.10.cloned.1.call-done
  3578.9 33.6 all-reduce.10.cloned.1.call-done
  3656.2 33.6 all-reduce.10.cloned.1.call-done
  3810.9 33.6 all-reduce.10.cloned.1.call-done
  3965.6 33.6 all-reduce.10.cloned.1.call-done
  4120.2 33.6 all-reduce.10.cloned.1.call-done
  4355.0 47.3 %all-reduce.8.cloned.1.call-done = (f32[1,400,1150]{2,1,0:T(8,128)}, f32[1,400,400]{2,1,0:T(8,128)}) async-done(((f32[1,400,1150]{2,1,0:T(8,128)}, f32[1,400,400]{2,1,0:T(8,128)}), (f32[1,400,1150]{2,1,0:T(8,128)}, f32[1,400,400]{2,1,0:T(8,128)})) %all-reduce.8.cloned.1.call-update) | async-done | bytes 2480016 | tf_op jit(solution)/shard_map/psum | solution.py:167
  4456.9 232.0 %reduce-scatter.4.cloned.1.call-done = f32[16,70,1150]{2,1,0:T(8,128)} async-done(((f32[64,70,1150]{2,1,0:T(8,128)}), f32[16,70,1150]{2,1,0:T(8,128)}) %reduce-scatter.4.cloned.1.call-update) | async-done | bytes 5152016 | tf_op jit(solution)/shard_map/reduce_scatter | solution.py:155
  (1397 shorter events, 3462.7 us)
Async XLA Ops:
  1561.2 40.5 all-reduce.10.cloned.1.call-start
  1679.0 38.7 all-reduce.10.cloned.1.call-start
  1717.6 38.7 all-reduce.10.cloned.1.call-start
  1833.6 38.7 all-reduce.10.cloned.1.call-start
  1872.3 38.7 all-reduce.10.cloned.1.call-start
  1988.3 38.7 all-reduce.10.cloned.1.call-start
  2027.0 38.7 all-reduce.10.cloned.1.call-start
  2143.0 38.7 all-reduce.10.cloned.1.call-start
  2181.7 38.7 all-reduce.10.cloned.1.call-start
  2297.7 38.7 all-reduce.10.cloned.1.call-start
  2336.4 38.7 all-reduce.10.cloned.1.call-start
  2452.4 38.7 all-reduce.10.cloned.1.call-start
  2491.0 38.7 all-reduce.10.cloned.1.call-start
  2607.0 38.7 all-reduce.10.cloned.1.call-start
  2645.7 38.7 all-reduce.10.cloned.1.call-start
  2761.7 38.7 all-reduce.10.cloned.1.call-start
  2800.4 38.7 all-reduce.10.cloned.1.call-start
  2916.4 38.7 all-reduce.10.cloned.1.call-start
  2955.1 38.7 all-reduce.10.cloned.1.call-start
  3071.1 38.7 all-reduce.10.cloned.1.call-start
  3109.7 38.7 all-reduce.10.cloned.1.call-start
  3225.7 38.7 all-reduce.10.cloned.1.call-start
  3264.4 38.7 all-reduce.10.cloned.1.call-start
  3380.4 38.7 all-reduce.10.cloned.1.call-start
  3419.1 38.7 all-reduce.10.cloned.1.call-start
  3573.8 38.7 all-reduce.10.cloned.1.call-start
  3689.8 38.7 all-reduce.10.cloned.1.call-start
  3728.5 38.7 all-reduce.10.cloned.1.call-start
  4153.8 38.7 all-reduce.10.cloned.1.call-start
  4192.5 38.7 all-reduce.10.cloned.1.call-start
  4307.5 94.8 %all-reduce.8.cloned.1.call-start = ((), (), s32[]{:S(2)}) async-start(), calls=%async_computation.6 | async-start | bytes 5324800 | tf_op jit(solution)/shard_map/psum | solution.py:167
  4318.8 370.2 %reduce-scatter.4.cloned.1.call-start = ((), (), s32[]{:S(2)}) async-start(), calls=%async_computation.3 | async-start | bytes 26542080 | tf_op jit(solution)/shard_map/reduce_scatter | solution.py:155
  (56 other events, 3749.7 us)
Sparse Core Ops, SparseCore 0:
  1565.7 35.9 all-reduce.9
  1644.8 34.1 all-reduce.9
  1683.5 34.1 all-reduce.9
  1722.1 34.1 all-reduce.9
  1799.5 34.1 all-reduce.9
  1838.1 34.1 all-reduce.9
  1876.8 34.1 all-reduce.9
  1954.1 34.1 all-reduce.9
  1992.8 34.1 all-reduce.9
  2031.5 34.1 all-reduce.9
  2108.8 34.1 all-reduce.9
  2147.5 34.1 all-reduce.9
  2186.2 34.1 all-reduce.9
  2263.5 34.1 all-reduce.9
  2302.2 34.1 all-reduce.9
  2340.9 34.1 all-reduce.9
  2418.2 34.1 all-reduce.9
  2456.9 34.1 all-reduce.9
  2495.5 34.1 all-reduce.9
  2572.9 34.1 all-reduce.9
  2611.5 34.1 all-reduce.9
  2727.5 34.1 all-reduce.9
  2882.2 34.1 all-reduce.9
  3036.9 34.1 all-reduce.9
  3191.6 34.1 all-reduce.9
  3346.2 34.1 all-reduce.9
  3500.9 34.1 all-reduce.9
  3655.6 34.1 all-reduce.9
  3810.3 34.1 all-reduce.9
  3965.0 34.1 all-reduce.9
  4119.6 34.1 all-reduce.9
  4335.8 353.1 reduce-scatter.3
  (39 shorter events, 1328.7 us)
Sparse Core Ops, SparseCore 1:
  4284.4 8.7 reduce-scatter.7
  4307.6 11.1 reduce-scatter.5
  4322.2 80.1 all-reduce.7
where the time goes:
time: 4720 us; the launch traced here: 4700 us
  waiting for transfers between devices  2650 us (56%)
  blocking collectives  1150 us (24%)
  local copies, waits for them, and re-layouts  459 us (10%)
  other arithmetic  285 us (6%)
  matrix products  144 us (3%)
    psum x70, waiting for transfers between devices, recur_back(): return lax.psum(partial_back, 'row')  2350 us
    all_gather x70, blocking collectives, full_gates(): return lax.all_gather(partial_gates, 'row', axis=1, tiled=True)  1100 us
    reduce_scatter x1, waiting for transfers between devices, local(): lax.psum_scatter(jnp.einsum('slr,rk->slk', grad_seq, input_gate_weight, p...  232 us
    another operation x142, other arithmetic  156 us
    dynamic_update_slice x140, local copies, waits for them, and re-layouts, local(): lax.scan(forward_step, start_state, projected)  102 us
  transfers between devices with their start and end apart: 75, of which 74 were waited for; matrix products, arithmetic and copies ran while one was open for 3% of the time, Pallas kernels for 0%

commit v1 on v0

--- a/solution.py
+++ b/solution.py
@@ -74,7 +74,12 @@
     def recur_back(pre_grad):
         own_rows = lax.dynamic_slice_in_dim(pre_grad, row_start, row_count, 1)
         partial_back = jnp.dot(own_rows, w_eff, preferred_element_type=jnp.float32)
-        return lax.psum(partial_back, "row")
+
+        def _bring_columns(frame_in):
+            heard = jnp.sum(lax.all_gather(frame_in, axis_name="row"), 0)
+            return heard
+
+        return _bring_columns(partial_back)
 
     def forward_step(carry, proj_step):
         cell_state, hidden_low = carry

time: 4720 us -> 3430 us (0.73)
  waiting for transfers between devices: 2650 us -> 300 us
  blocking collectives: 1150 us -> 2260 us
    psum x70 -> x0, waiting for transfers between devices: 2350 us -> none  [recur_back(): return lax.psum(partial_back, 'row')]
    all_gather x0 -> x70, blocking collectives: none -> 1100 us  [_bring_columns(): heard = jnp.sum(lax.all_gather(frame_in, axis_name='row'), 0)]
  transfers between devices with their start and end apart: 75 -> 5, of which waited for: 74 -> 4; matrix products, arithmetic and copies ran while one was open for 3% -> 2% of each run, Pallas kernels for 0% -> 0%
where the time goes in v1:
time: 3430 us; the launch traced here: 3420 us
  blocking collectives  2260 us (66%)
  local copies, waits for them, and re-layouts  454 us (13%)
  waiting for transfers between devices  300 us (9%)
  other arithmetic  285 us (8%)
  matrix products  97.2 us (3%)
    all_gather x70, blocking collectives, full_gates(): return lax.all_gather(partial_gates, 'row', axis=1, tiled=True)  1110 us
    all_gather x70, blocking collectives, _bring_columns(): heard = jnp.sum(lax.all_gather(frame_in, axis_name='row'), 0)  1100 us
    reduce_scatter x1, waiting for transfers between devices, local(): lax.psum_scatter(jnp.einsum('slr,rk->slk', grad_seq, input_gate_weight, p...  234 us
    another operation x142, other arithmetic  152 us
    dynamic_update_slice x140, local copies, waits for them, and re-layouts, local(): lax.scan(forward_step, start_state, projected)  102 us
    dynamic_slice x70, local copies, waits for them, and re-layouts, local(): lax.scan(forward_step, start_state, projected)  93.5 us
    squeeze x70, local copies, waits for them, and re-layouts, local(): lax.scan(backward_step, (zero_state, zero_state), (direct_grad, activatio...  72.8 us
  transfers between devices with their start and end apart: 5, of which 4 were waited for; matrix products, arithmetic and copies ran while one was open for 2% of the time, Pallas kernels for 0%

profile of v1, /device:TPU:0, one launch (start us, length us, event | category | flops | bytes accessed | tf_op | source)
XLA Modules:
  0.0 3416.6 jit_solution(10839606858315069539)
XLA Ops:
  32.9 1468.5 %while.38 = (s32[]{:T(128)}, f32[64,400]{1,0:T(8,128)S(1)}, bf16[64,400]{1,0:T(8,128)(2,1)S(1)}, f32[70,64,1600]{2,1,0:T(8,128)}, f32[70,64,400]{2,1,0:T(8,128)}...) while((s32[]{:T(128)}, f32[64,400]{1,0:T(8,128)S(1)}, ...), condition=%wide.region_6.7_spmd.clone, body=%wide.region_5.6_spmd.clone.sunk | while | flops 21171204 | bytes 6539380 | solution.py:94
  34.6 17.4 all-gather.6
  140.4 16.6 all-gather.6
  162.2 16.5 all-gather.6
  267.4 16.6 all-gather.6
  289.1 16.6 all-gather.6
  394.5 16.5 all-gather.6
  416.1 16.6 all-gather.6
  499.7 16.4 all-gather.6
  521.3 16.6 all-gather.6
  543.0 16.7 all-gather.6
  648.2 16.4 all-gather.6
  669.7 16.6 all-gather.6
  774.6 16.8 all-gather.6
  796.6 16.5 all-gather.6
  901.7 16.6 all-gather.6
  923.4 16.6 all-gather.6
  1028.6 16.7 all-gather.6
  1050.5 16.5 all-gather.6
  1565.2 1413.2 %while.39 = (s32[]{:T(128)}, f32[64,400]{1,0:T(8,128)S(1)}, f32[64,400]{1,0:T(8,128)S(1)}, bf16[70,64,400]{2,1,0:T(8,128)(2,1)}, f32[70,64,400]{2,1,0:T(8,128)},...) while((s32[]{:T(128)}, f32[64,400]{1,0:T(8,128)S(1)}, ...), condition=%wide.region_9.10_spmd.clone, body=%wide.region_7.9_spmd.clone.sunk | while | flops 21273604 | bytes 4586163 | solution.py:136
  1569.6 16.9 all-gather.7
  1672.1 16.6 all-gather.7
  1935.0 16.5 all-gather.7
  2037.1 16.7 all-gather.7
  2159.6 16.6 all-gather.7
  2403.4 16.7 all-gather.7
  2647.3 16.7 all-gather.7
  3031.3 16.5 fusion.34
  3067.1 48.0 %all-reduce.7.cloned.1.call-done = (f32[1,400,1150]{2,1,0:T(8,128)}, f32[1,400,400]{2,1,0:T(8,128)}) async-done(((f32[1,400,1150]{2,1,0:T(8,128)}, f32[1,400,400]{2,1,0:T(8,128)}), (f32[1,400,1150]{2,1,0:T(8,128)}, f32[1,400,400]{2,1,0:T(8,128)})) %all-reduce.7.cloned.1.call-update) | async-done | bytes 2480016 | tf_op jit(solution)/shard_map/psum | solution.py:172
  3120.5 17.5 concatenate.28
  3148.5 18.6 psum.39
  3167.0 233.9 %reduce-scatter.4.cloned.1.call-done = f32[16,70,1150]{2,1,0:T(8,128)} async-done(((f32[64,70,1150]{2,1,0:T(8,128)}), f32[16,70,1150]{2,1,0:T(8,128)}) %reduce-scatter.4.cloned.1.call-update) | async-done | bytes 5152016 | tf_op jit(solution)/shard_map/reduce_scatter | solution.py:160
  (1327 shorter events, 2643.5 us)
Async XLA Ops:
  8.0 13.6 copy-start
  8.0 3008.5 %reduce-scatter.8.cloned.1.call-start = ((), (), s32[]{:S(2)}) async-start(), calls=%async_computation.5 | async-start | bytes 2457600 | tf_op jit(solution)/shard_map/reduce_scatter | solution.py:169
  10.7 10.7 copy-start.4
  10.7 10.7 copy-start.6
  10.7 10.9 copy-start.10
  32.9 1468.5 %copy-start.11 = (s32[64]{0:T(128)S(1)}, s32[64]{0:T(128)}, u32[]{:S(2)}) copy-start(s32[64]{0:T(128)} %param.18) | copy-start | bytes 772
  1501.6 25.0 copy-start.9
  1533.7 4.6 copy-start.7
  2978.4 7.5 copy-start.1
  2978.4 7.4 copy-start.5
  2993.0 38.0 %reduce-scatter.6.cloned.1.call-start = ((), (), s32[]{:S(2)}) async-start(), calls=%async_computation.4 | async-start | bytes 5529600 | tf_op jit(solution)/shard_map/reduce_scatter | solution.py:168
  3016.4 98.7 %all-reduce.7.cloned.1.call-start = ((), (), s32[]{:S(2)}) async-start(), calls=%async_computation.6 | async-start | bytes 5324800 | tf_op jit(solution)/shard_map/psum | solution.py:172
  3031.0 370.0 %reduce-scatter.4.cloned.1.call-start = ((), (), s32[]{:S(2)}) async-start(), calls=%async_computation.3 | async-start | bytes 26542080 | tf_op jit(solution)/shard_map/reduce_scatter | solution.py:160
  3047.8 0.7 copy-start.12
  3067.1 336.8 %copy-start.8 = (f32[1,400]{1,0:T(1,128)}, f32[1,400]{1,0:T(1,128)S(1)}, u32[]{:S(2)}) copy-start(f32[1,400]{1,0:T(1,128)S(1)} %psum.38) | copy-start | bytes 4804
  3140.9 3.1 collective-permute-start
  3167.0 240.1 %copy-start.2 = (f32[1,400,1150]{2,1,0:T(8,128)S(1)}, f32[1,400,1150]{2,1,0:T(8,128)}, u32[]{:S(2)}) copy-start(f32[1,400,1150]{2,1,0:T(8,128)} %get-tuple-element.655) | copy-start | bytes 5520004
  3403.8 4.5 copy-start.3
Sparse Core Ops, SparseCore 0:
  2993.1 12.1 reduce-scatter.7
  3016.5 14.4 reduce-scatter.5
  3034.5 80.5 all-reduce.6
Sparse Core Ops, SparseCore 1:
  3047.9 353.0 reduce-scatter.3
